TPU v7x, 512 devices: a whole 4x4x16 slice. The times are simulated.
512 devices in a mesh: dp: 32 (over x_lo, z), mp: 16 (over y, x_hi, core).
Axes of the slice: x: 4 (x_hi: 2, x_lo: 2; x = x_hi * 2 + x_lo), y: 4, z: 16, core: 2. Of those that a mesh axis runs over, the one named last changes fastest.
Arguments:
- activations: bfloat16 [32, 1024, 512], P('dp', 'mp'), may hold values from -6 to 6
- filters: bfloat16 [27, 1024, 1024], P(None, 'mp', 'dp'), may hold values from -0.0390625 to 0.0390625
- bias: float32 [1024], P('mp'), may hold values from -3 to 3
Outputs:
- features: bfloat16 [32, 1024, 512], P('dp', 'mp')
All inputs are finite; a program needn't handle non-finite values.
Results may differ from a plain program's by a relative error of at most 0.001.
Values may be sent and summed in bfloat16 or wider, within the bound.
No kernel may reach another device: no remote copies, remote signals or barrier semaphores. Data moves between devices by JAX's collectives and lax.ppermute only.
A program may use at most 128 MiB of HBM per device.

v0:
```python
import jax
import jax.numpy as jnp
from jax import lax
from jax.sharding import PartitionSpec as P

SX = 2
SY = 16
SZ = 16


def stacked_taps(values):
    cells = SX * SY * SZ
    margin = SY * SZ + SZ + 1
    extended = jnp.pad(values, ((0, 0), (margin, margin)))
    place = jnp.arange(cells, dtype=jnp.int32)
    first_pos = place // (SY * SZ)
    second_pos = place // SZ % SY
    third_pos = place % SZ
    copies = []
    for off_a in (-1, 0, 1):
        for off_b in (-1, 0, 1):
            for off_c in (-1, 0, 1):
                offset = off_a * SY * SZ + off_b * SZ + off_c
                moved = extended[:, margin + offset : margin + offset + cells]
                first = first_pos + off_a
                second = second_pos + off_b
                third = third_pos + off_c
                inside = (
                    (first >= 0)
                    & (first < SX)
                    & (second >= 0)
                    & (second < SY)
                    & (third >= 0)
                    & (third < SZ)
                )
                copies.append(jnp.where(inside[None, :], moved, jnp.zeros_like(moved)))
    return jnp.concatenate(copies, axis=0)


def add_taps(weights, inputs):
    taps_count, out_rows, chans = weights.shape
    flat_weights = jnp.transpose(weights, (1, 0, 2)).reshape(out_rows, taps_count * chans)
    return jnp.dot(flat_weights, stacked_taps(inputs), preferred_element_type=jnp.float32)


def per_device(activations, filters, bias):
    all_filters = lax.all_gather(filters, "dp", axis=2, tiled=True)
    summed = add_taps(all_filters, lax.all_gather(activations, "mp", axis=1, tiled=True)[0])
    value = summed + bias[:, None]
    result = jnp.where(value > 0, value, 0.3 * value).astype(jnp.bfloat16)
    return result[None]


def solution(mesh):
    in_specs = (P("dp", "mp", None), P(None, "mp", "dp"), P("mp"))
    out_specs = P("dp", "mp", None)
    return jax.shard_map(
        per_device, mesh=mesh, in_specs=in_specs, out_specs=out_specs, check_vma=False
    )
```

profile of v0, /device:TPU:8, one launch (start us, length us, event | category | flops | bytes accessed | tf_op | source)
XLA Modules:
  0.0 245.5 jit_solution(933689072745846719)
XLA Ops:
  6.5 0.0 all-gather.3.cloned.1.call-start
  6.5 0.7 all-gather.3.cloned.1.call-update
  7.3 0.0 all-gather.5.cloned.1.call-start
  7.3 0.7 all-gather.5.cloned.1.call-update
  8.4 66.4 %all-gather.3.cloned.1.call-done = bf16[1,1024,512]{2,1,0:T(8,128)(2,1)} async-done(((bf16[1,64,512]{2,1,0:T(8,128)(2,1)}), bf16[1,1024,512]{2,1,0:T(8,128)(2,1)}) %all-gather.3.cloned.1.call-update) | async-done | bytes 1048592 | tf_op jit(solution)/shard_map/all_gather | solution.py:48
  74.8 0.0 copy-start
  74.8 0.0 copy-start.1
  74.8 2.3 fusion.2
  77.2 2.4 fusion.4
  79.6 2.4 fusion.6
  82.0 2.4 fusion.8
  84.4 2.3 fusion.10
  86.7 2.6 %fusion.12 = bf16[27648,512]{1,0:T(8,128)(2,1)} fusion(bf16[27648,512]{1,0:T(8,128)(2,1)} %fusion.10, bf16[1024,512]{1,0:T(8,128)(2,1)} %bitcast.22, pred[512]{0:T(512)(128)(4,1)S(1)} %and_and_fusion.28), kind=kLoop, calls=%fused_computation.39 | loop fusion | flops 524288 | bytes 2097664
  89.3 2.6 %fusion.14 = bf16[27648,512]{1,0:T(8,128)(2,1)} fusion(bf16[27648,512]{1,0:T(8,128)(2,1)} %fusion.12, bf16[1024,512]{1,0:T(8,128)(2,1)} %bitcast.23, pred[512]{0:T(512)(128)(4,1)S(1)} %and_and_fusion.26), kind=kLoop, calls=%fused_computation.41 | loop fusion | flops 524288 | bytes 2097664
  91.9 2.7 %fusion.16 = bf16[27648,512]{1,0:T(8,128)(2,1)} fusion(bf16[27648,512]{1,0:T(8,128)(2,1)} %fusion.14, bf16[1024,512]{1,0:T(8,128)(2,1)} %bitcast.24, pred[512]{0:T(512)(128)(4,1)S(1)} %and_and_fusion.25), kind=kLoop, calls=%fused_computation.43 | loop fusion | flops 524288 | bytes 2097664
  94.5 2.6 %fusion.18 = bf16[27648,512]{1,0:T(8,128)(2,1)} fusion(bf16[27648,512]{1,0:T(8,128)(2,1)} %fusion.16, bf16[1024,512]{1,0:T(8,128)(2,1)} %bitcast.25, pred[512]{0:T(512)(128)(4,1)S(1)} %and_and_fusion.24), kind=kLoop, calls=%fused_computation.45 | loop fusion | flops 524288 | bytes 2097664
  97.2 2.7 %fusion.20 = bf16[27648,512]{1,0:T(8,128)(2,1)} fusion(bf16[27648,512]{1,0:T(8,128)(2,1)} %fusion.18, bf16[1024,512]{1,0:T(8,128)(2,1)} %bitcast.26, pred[512]{0:T(512)(128)(4,1)S(1)} %and_and_fusion.22), kind=kLoop, calls=%fused_computation.47 | loop fusion | flops 524288 | bytes 2097664
  99.9 2.8 %fusion.22 = bf16[27648,512]{1,0:T(8,128)(2,1)} fusion(bf16[27648,512]{1,0:T(8,128)(2,1)} %fusion.20, bf16[1024,512]{1,0:T(8,128)(2,1)} %bitcast.27, pred[512]{0:T(512)(128)(4,1)S(1)} %and_and_fusion.21), kind=kLoop, calls=%fused_computation.49 | loop fusion | flops 524288 | bytes 2097664
  102.6 2.8 %fusion.24 = bf16[27648,512]{1,0:T(8,128)(2,1)} fusion(bf16[27648,512]{1,0:T(8,128)(2,1)} %fusion.22, bf16[1024,512]{1,0:T(8,128)(2,1)} %bitcast.28, pred[512]{0:T(512)(128)(4,1)S(1)} %and_and_fusion.20), kind=kLoop, calls=%fused_computation.51 | loop fusion | flops 524288 | bytes 2097664
  105.4 2.8 %fusion.26 = bf16[27648,512]{1,0:T(8,128)(2,1)} fusion(bf16[27648,512]{1,0:T(8,128)(2,1)} %fusion.24, bf16[1024,512]{1,0:T(8,128)(2,1)} %bitcast.29, pred[512]{0:T(512)(128)(4,1)S(1)} %and_and_fusion.18), kind=kLoop, calls=%fused_computation.53 | loop fusion | flops 524288 | bytes 2097664
  108.2 2.4 select_dynamic-update-slice_fusion
  110.6 0.0 copy-done
  110.6 1.5 fusion.28
  112.1 1.5 fusion.30
  113.6 1.5 fusion.32
  115.1 1.5 fusion.34
  116.6 1.3 fusion.36
  118.0 1.3 fusion.38
  119.3 1.3 fusion.40
  120.6 1.4 fusion.42
  122.0 1.1 fusion.44
  123.1 1.3 fusion.46
  124.4 1.3 fusion.48
  125.7 1.2 fusion.50
  126.9 1.2 fusion.52
  128.1 94.0 %all-gather.5.cloned.1.call-done = bf16[27,64,1024]{1,2,0:T(8,128)(2,1)} async-done(((bf16[27,64,32]{1,2,0:T(8,128)(2,1)}), bf16[27,64,1024]{1,2,0:T(8,128)(2,1)}) %all-gather.5.cloned.1.call-update) | async-done | bytes 3538960 | tf_op jit(solution)/shard_map/all_gather | solution.py:47
  222.2 0.0 copy-done.1
  222.2 16.5 %fusion.54 = bf16[1,64,512]{2,1,0:T(8,128)(2,1)} fusion(bf16[27648,512]{1,0:T(8,128)(2,1)} %fusion.52, bf16[64,27648]{0,1:T(8,128)(2,1)} %bitcast.43, f32[64]{0:T(128)S(1)} %copy-done.1), kind=kOutput, calls=%fused_computation.83 | convolution fusion | flops 1812103168 | bytes 31916288 | tf_op jit(solution)/shard_map/dot_general | solution.py:43
  (27 shorter events, 0.3 us)
Async XLA Ops:
  6.5 68.3 %all-gather.3.cloned.1.call-start = ((), (), s32[]{:S(2)}) async-start(), calls=%async_computation | async-start | bytes 1114112 | tf_op jit(solution)/shard_map/all_gather | solution.py:48
  7.3 214.9 %all-gather.5.cloned.1.call-start = ((), (), s32[]{:S(2)}) async-start(), calls=%async_computation.1 | async-start | bytes 7299072 | tf_op jit(solution)/shard_map/all_gather | solution.py:47
  74.8 35.8 %copy-start = (bf16[1,1024,512]{2,1,0:T(8,128)(2,1)S(1)}, bf16[1,1024,512]{2,1,0:T(8,128)(2,1)}, u32[]{:S(2)}) copy-start(bf16[1,1024,512]{2,1,0:T(8,128)(2,1)} %all-gather.3.cloned.1.call-done) | copy-start | bytes 3145732
  74.8 147.3 %copy-start.1 = (f32[64]{0:T(128)S(1)}, f32[64]{0:T(128)}, u32[]{:S(2)}) copy-start(f32[64]{0:T(128)} %param.5) | copy-start | bytes 772
Sparse Core Ops, SparseCore 0:
  10.7 64.1 all-gather.2
  76.9 145.1 all-gather.4
where the time goes:
time: 246 us
  waiting for transfers between devices  162 us (66%)
  other arithmetic  53.6 us (22%)
  matrix products  16.5 us (7%)
  between operations  13.5 us (5%)
    all_gather x1, waiting for transfers between devices, per_device(): all_filters = lax.all_gather(filters, 'dp', axis=2, tiled=True)  94 us
    all_gather x1, waiting for transfers between devices, per_device(): lax.all_gather(activations, 'mp', axis=1, tiled=True)[0]  66.4 us
    unnamed x26, other arithmetic  52 us
    dot_general x1, matrix products, add_taps(): jnp.dot(flat_weights, stacked_taps(inputs), preferred_element_type=jnp.fl...  16.5 us
  transfers between devices with their start and end apart: 2, of which 2 were waited for; matrix products, arithmetic and copies ran while one was open for 22% of the time, Pallas kernels for 0%

commit v1 on v0

--- a/solution.py
+++ b/solution.py
@@ -45,7 +45,12 @@
 
 def per_device(activations, filters, bias):
     all_filters = lax.all_gather(filters, "dp", axis=2, tiled=True)
-    summed = add_taps(all_filters, lax.all_gather(activations, "mp", axis=1, tiled=True)[0])
+    summed = add_taps(
+        all_filters,
+        jnp.concatenate(
+            lax.all_to_all(jnp.stack([activations] * lax.axis_size("mp")), "mp", 0, 0), axis=1
+        )[0],
+    )
     value = summed + bias[:, None]
     result = jnp.where(value > 0, value, 0.3 * value).astype(jnp.bfloat16)
     return result[None]

time: 246 us -> 193 us (0.78)
  waiting for transfers between devices: 162 us -> 114 us
  other arithmetic: 53.6 us -> 36.7 us
  starting transfers between devices: 0.04 us -> 9.29 us
    all_gather x1 -> x0, waiting for transfers between devices: 66.4 us -> none  [per_device(): lax.all_gather(activations, 'mp', axis=1, tiled=True)[0]]
    unnamed x26, other arithmetic: 52 us -> 35.2 us
    all_to_all x0 -> x1, waiting for transfers between devices: none -> 14.2 us  [per_device(): lax.all_to_all(jnp.stack([activations] * lax.axis_size('mp')), 'mp', 0, 0)]
    all_to_all x0 -> x1, starting transfers between devices: none -> 9.26 us  [per_device(): lax.all_to_all(jnp.stack([activations] * lax.axis_size('mp')), 'mp', 0, 0)]
    all_gather x1, waiting for transfers between devices: 94 us -> 99.4 us  [per_device(): all_filters = lax.all_gather(filters, 'dp', axis=2, tiled=True)]
  transfers between devices with their start and end apart: 2 -> 2, of which waited for: 2 -> 2; matrix products, arithmetic and copies ran while one was open for 22% -> 19% of each run, Pallas kernels for 0% -> 0%
where the time goes in v1:
time: 193 us; the launch traced here: 192 us
  waiting for transfers between devices  114 us (59%)
  other arithmetic  36.7 us (19%)
  matrix products  16.5 us (9%)
  between operations  13.5 us (7%)
  starting transfers between devices  9.29 us (5%)
    all_gather x1, waiting for transfers between devices, per_device(): all_filters = lax.all_gather(filters, 'dp', axis=2, tiled=True)  99.4 us
    unnamed x26, other arithmetic  35.2 us
    dot_general x1, matrix products, add_taps(): jnp.dot(flat_weights, stacked_taps(inputs), preferred_element_type=jnp.fl...  16.5 us
    all_to_all x1, waiting for transfers between devices, per_device(): lax.all_to_all(jnp.stack([activations] * lax.axis_size('mp')), 'mp', 0, 0)  14.2 us
    all_to_all x1, starting transfers between devices, per_device(): lax.all_to_all(jnp.stack([activations] * lax.axis_size('mp')), 'mp', 0, 0)  9.26 us
  transfers between devices with their start and end apart: 2, of which 2 were waited for; matrix products, arithmetic and copies ran while one was open for 19% of the time, Pallas kernels for 0%

profile of v1, /device:TPU:8, one launch (start us, length us, event | category | flops | bytes accessed | tf_op | source)
XLA Modules:
  0.0 192.3 jit_solution(8989374907668469236)
XLA Ops:
  6.5 1.9 stack.2
  8.4 9.3 %all-to-all-start = ((bf16[16,1,64,512]{3,2,1,0:T(8,128)(2,1)}), bf16[16,1,64,512]{3,2,1,0:T(8,128)(2,1)S(1)}, u32[]{:S(2)}, u32[]{:S(2)}) async-start(bf16[16,1,64,512]{3,2,1,0:T(8,128)(2,1)} %stack.2), calls=%async_computation | async-start | bytes 2097152 | tf_op jit(solution)/shard_map/all_to_all | solution.py:51
  17.7 0.0 all-gather.2.cloned.1.call-start
  17.8 0.7 all-gather.2.cloned.1.call-update
  18.9 14.2 %all-to-all-done = bf16[16,1,64,512]{3,2,1,0:T(8,128)(2,1)S(1)} async-done(((bf16[16,1,64,512]{3,2,1,0:T(8,128)(2,1)}), bf16[16,1,64,512]{3,2,1,0:T(8,128)(2,1)S(1)}, u32[]{:S(2)}, u32[]{:S(2)}) %all-to-all-start) | async-done | bytes 1048608 | tf_op jit(solution)/shard_map/all_to_all | solution.py:51
  33.1 0.0 copy-start
  33.1 1.2 fusion.2
  34.3 1.3 fusion.4
  35.6 1.2 fusion.6
  36.8 1.2 fusion.8
  38.0 1.1 fusion.10
  39.1 1.4 fusion.12
  40.5 1.4 fusion.14
  41.9 1.4 fusion.16
  43.3 1.4 fusion.18
  44.7 1.5 fusion.20
  46.2 1.5 fusion.22
  47.8 1.5 fusion.24
  49.3 1.6 fusion.26
  50.9 1.2 select_dynamic-update-slice_fusion
  52.0 1.5 fusion.28
  53.6 1.5 fusion.30
  55.0 1.5 fusion.32
  56.5 1.5 fusion.34
  58.1 1.3 fusion.36
  59.4 1.3 fusion.38
  60.7 1.3 fusion.40
  62.0 1.3 fusion.42
  63.4 1.1 fusion.44
  64.5 1.3 fusion.46
  65.7 1.3 fusion.48
  67.0 1.2 fusion.50
  68.3 1.2 fusion.52
  69.5 99.4 %all-gather.2.cloned.1.call-done = bf16[27,64,1024]{1,2,0:T(8,128)(2,1)} async-done(((bf16[27,64,32]{1,2,0:T(8,128)(2,1)}), bf16[27,64,1024]{1,2,0:T(8,128)(2,1)}) %all-gather.2.cloned.1.call-update) | async-done | bytes 3538960 | tf_op jit(solution)/shard_map/all_gather | solution.py:47
  168.9 0.0 copy-done
  168.9 16.5 %fusion.54 = bf16[1,64,512]{2,1,0:T(8,128)(2,1)} fusion(bf16[27648,512]{1,0:T(8,128)(2,1)} %fusion.52, bf16[64,27648]{0,1:T(8,128)(2,1)} %bitcast.44, f32[64]{0:T(128)S(1)} %copy-done), kind=kOutput, calls=%fused_computation.83 | convolution fusion | flops 1812103168 | bytes 31916288 | tf_op jit(solution)/shard_map/dot_general | solution.py:43
  (27 shorter events, 0.3 us)
Async XLA Ops:
  8.4 24.6 %all-to-all-start = ((bf16[16,1,64,512]{3,2,1,0:T(8,128)(2,1)}), bf16[16,1,64,512]{3,2,1,0:T(8,128)(2,1)S(1)}, u32[]{:S(2)}, u32[]{:S(2)}) async-start(bf16[16,1,64,512]{3,2,1,0:T(8,128)(2,1)} %stack.2), calls=%async_computation | async-start | bytes 2097152 | tf_op jit(solution)/shard_map/all_to_all | solution.py:51
  17.7 151.2 %all-gather.2.cloned.1.call-start = ((), (), s32[]{:S(2)}) async-start(), calls=%async_computation.1 | async-start | bytes 7299072 | tf_op jit(solution)/shard_map/all_gather | solution.py:47
  33.1 135.9 %copy-start = (f32[64]{0:T(128)S(1)}, f32[64]{0:T(128)}, u32[]{:S(2)}) copy-start(f32[64]{0:T(128)} %param.5) | copy-start | bytes 772
Sparse Core Ops, SparseCore 0:
  20.6 148.2 all-gather.1
